TPU v7x, 32 devices: a whole 2x2x4 slice. The times are simulated.
32 devices in a mesh: dp: 8 (over z, core), tensor: 4 (over y, x).
Axes of the slice: x: 2, y: 2, z: 4, core: 2. Of those that a mesh axis runs over, the one named last changes fastest.
Arguments:
- layer_input: bfloat16 [8192, 2048], P(('dp', 'tensor')), may hold values from -6 to 6
- norm1_gain: bfloat16 [2048], P('dp'), may hold values from 0.25 to 1.75
- norm1_bias: bfloat16 [2048], P('dp'), may hold values from -3 to 3
- qkv_weight: bfloat16 [3, 2048, 2048], P(None, 'dp', 'tensor'), may hold values from -0.125 to 0.125
- qkv_bias: bfloat16 [3, 2048], P(None, ('tensor', 'dp')), may hold values from -6 to 6
- out_weight: bfloat16 [2048, 2048], P('tensor', 'dp'), may hold values from -0.5 to 0.5
- norm2_gain: bfloat16 [2048], P('dp'), may hold values from 0.25 to 1.75
- norm2_bias: bfloat16 [2048], P('dp'), may hold values from -3 to 3
- gate_up_weight: bfloat16 [2, 2048, 5632], P(None, 'dp', 'tensor'), may hold values from -0.125 to 0.125
- down_weight: bfloat16 [5632, 2048], P('tensor', 'dp'), may hold values from -0.15625 to 0.15625
- out_cotangent: bfloat16 [8192, 2048], P(('dp', 'tensor')), may hold values from -6 to 6
Outputs:
- layer_output: bfloat16 [8192, 2048], P(('dp', 'tensor'))
- grad_input: float32 [8192, 2048], P(('dp', 'tensor'))
- grad_norm1_gain: float32 [2048], P('dp')
- grad_norm1_bias: float32 [2048], P('dp')
- grad_qkv_weight: float32 [3, 2048, 2048], P(None, 'dp', 'tensor')
- grad_qkv_bias: float32 [3, 2048], P(None, ('tensor', 'dp'))
- grad_out_weight: float32 [2048, 2048], P('tensor', 'dp')
- grad_norm2_gain: float32 [2048], P('dp')
- grad_norm2_bias: float32 [2048], P('dp')
- grad_gate_up_weight: float32 [2, 2048, 5632], P(None, 'dp', 'tensor')
- grad_down_weight: float32 [5632, 2048], P('tensor', 'dp')
All inputs are finite; a program needn't handle non-finite values.
Results may differ from a plain program's by a relative error of at most 0.025.
The roundings to bfloat16 on the way count: a program that leaves them out, or rounds other values in their place, can miss the bound.
Values may be sent and summed in bfloat16 or wider, within the bound.
No kernel may reach another device: no remote copies, remote signals or barrier semaphores. Data moves between devices by JAX's collectives and lax.ppermute only.
A program may use at most 192 MiB of HBM per device.

v0:
```python
import jax
import jax.numpy as jnp
from jax import lax
from jax.sharding import PartitionSpec as P

HEAD_DIM = 64
ROT = 16
SEQ_LEN = 512
epsilon = 1e-05


def layer_norm(values):
    row_mean = jnp.mean(values, axis=-1, keepdims=True)
    centered = values - row_mean
    inv_sigma = lax.rsqrt(jnp.mean(centered * centered, axis=-1, keepdims=True) + epsilon)
    return (centered * inv_sigma, inv_sigma)


def norm_back(grad_hat, normed, inv_sigma):
    return inv_sigma * (
        grad_hat
        - jnp.mean(grad_hat, axis=-1, keepdims=True)
        - normed * jnp.mean(grad_hat * normed, axis=-1, keepdims=True)
    )


def rotary_tables(length, rot_dims):
    half_rot = rot_dims // 2
    frequency = 10000.0 ** (-(2.0 * jnp.arange(half_rot, dtype=jnp.float32)) / rot_dims)
    angles = jnp.arange(length, dtype=jnp.float32)[:, None] * frequency[None, :]
    return (jnp.cos(angles)[:, None, :], jnp.sin(angles)[:, None, :])


def rotate(tensor, cosine_table, sine_table, rot_dims):
    half_rot = rot_dims // 2
    lower_half = tensor[..., :half_rot]
    upper_half = tensor[..., half_rot:rot_dims]
    return jnp.concatenate(
        [
            lower_half * cosine_table - upper_half * sine_table,
            upper_half * cosine_table + lower_half * sine_table,
            tensor[..., rot_dims:],
        ],
        axis=-1,
    )


def unrotate(tensor, cosine_table, sine_table, rot_dims):
    half_rot = rot_dims // 2
    lower_half = tensor[..., :half_rot]
    upper_half = tensor[..., half_rot:rot_dims]
    return jnp.concatenate(
        [
            lower_half * cosine_table + upper_half * sine_table,
            upper_half * cosine_table - lower_half * sine_table,
            tensor[..., rot_dims:],
        ],
        axis=-1,
    )


def causal_mask(length):
    places = jnp.arange(length)
    return places[:, None] >= places[None, :]


def attention_params(norm1_gain, norm1_bias, qkv_weight, qkv_bias, out_weight):
    return (
        lax.all_gather(norm1_gain, "dp", axis=0, tiled=True),
        lax.all_gather(norm1_bias, "dp", axis=0, tiled=True),
        lax.all_gather(qkv_weight, "dp", axis=1, tiled=True),
        lax.all_gather(qkv_bias, "dp", axis=1, tiled=True),
        lax.all_gather(out_weight, "dp", axis=1, tiled=True),
    )


def mlp_params(norm2_gain, norm2_bias, gate_up_weight, down_weight):
    return (
        lax.all_gather(norm2_gain, "dp", axis=0, tiled=True),
        lax.all_gather(norm2_bias, "dp", axis=0, tiled=True),
        lax.all_gather(gate_up_weight, "dp", axis=1, tiled=True),
        lax.all_gather(down_weight, "dp", axis=1, tiled=True),
    )


def collect_rows(row_block):
    return lax.all_gather(row_block, "tensor", axis=0, tiled=True)


def spread_rows(term_fn, row_total):
    return lax.psum_scatter(
        term_fn(jnp.int32(0), row_total * lax.axis_size("tensor")).astype(jnp.bfloat16),
        "tensor",
        scatter_dimension=0,
        tiled=True,
    ).astype(jnp.float32)


def shards(
    layer_input,
    norm1_gain,
    norm1_bias,
    qkv_weight,
    qkv_bias,
    out_weight,
    norm2_gain,
    norm2_bias,
    gate_up_weight,
    down_weight,
    out_cotangent,
):
    local_rows = layer_input.shape[0]
    score_scale = HEAD_DIM ** (-0.5)
    cosine_table, sine_table = rotary_tables(SEQ_LEN, ROT)
    causal = causal_mask(SEQ_LEN)
    gain_one, bias_one, qkv_local, bias_local, out_local = attention_params(
        norm1_gain, norm1_bias, qkv_weight, qkv_bias, out_weight
    )
    x_float = layer_input.astype(jnp.float32)
    hat_one, inv_one = layer_norm(x_float)
    normed_one = (hat_one * gain_one.astype(jnp.float32) + bias_one.astype(jnp.float32)).astype(
        jnp.bfloat16
    )
    rows_one = collect_rows(normed_one)
    group_rows = rows_one.shape[0]
    seq_count = group_rows // SEQ_LEN
    head_cols = qkv_local.shape[2]
    heads_here = head_cols // HEAD_DIM
    qkv_all = (
        jnp.einsum("rd,cdk->crk", rows_one, qkv_local, preferred_element_type=jnp.float32)
        + bias_local.astype(jnp.float32)[:, None, :]
    )
    qkv_all = qkv_all.reshape(3, seq_count, SEQ_LEN, heads_here, HEAD_DIM)
    query_rot = rotate(qkv_all[0], cosine_table, sine_table, ROT).astype(jnp.bfloat16)
    key_rot = rotate(qkv_all[1], cosine_table, sine_table, ROT).astype(jnp.bfloat16)
    value_heads = qkv_all[2].astype(jnp.bfloat16)

    def attend(pieces):
        query_seq, key_seq, value_seq = pieces
        scores = (
            jnp.einsum("qhd,khd->hqk", query_seq, key_seq, preferred_element_type=jnp.float32)
            * score_scale
        )
        scores = jnp.where(causal, scores, -jnp.inf)
        row_top = jnp.max(scores, axis=-1, keepdims=True)
        log_total = row_top + jnp.log(jnp.sum(jnp.exp(scores - row_top), axis=-1, keepdims=True))
        prob_low = jnp.exp(scores - log_total).astype(jnp.bfloat16)
        context_seq = jnp.einsum(
            "hqk,khd->qhd", prob_low, value_seq, preferred_element_type=jnp.float32
        ).astype(jnp.bfloat16)
        return (context_seq, log_total[..., 0])

    context, log_totals = lax.map(attend, (query_rot, key_rot, value_heads))
    context_rows = context.reshape(group_rows, head_cols)

    def attn_term(row_start, row_count):
        return jnp.dot(context_rows, out_local, preferred_element_type=jnp.float32)

    residual = x_float + spread_rows(attn_term, local_rows)
    gain_two, bias_two, gate_up_local, down_local = mlp_params(
        norm2_gain, norm2_bias, gate_up_weight, down_weight
    )
    hat_two, inv_two = layer_norm(residual)
    normed_two = (hat_two * gain_two.astype(jnp.float32) + bias_two.astype(jnp.float32)).astype(
        jnp.bfloat16
    )
    rows_two = collect_rows(normed_two)
    gate_proj = jnp.dot(rows_two, gate_up_local[0], preferred_element_type=jnp.float32)
    up_proj = jnp.dot(rows_two, gate_up_local[1], preferred_element_type=jnp.float32)
    sigmoid_gate = jax.nn.sigmoid(gate_proj)
    silu_gate = gate_proj * sigmoid_gate
    activation = (silu_gate * up_proj).astype(jnp.bfloat16)

    def mlp_term(row_start, row_count):
        return jnp.dot(activation, down_local, preferred_element_type=jnp.float32)

    layer_output = (residual + spread_rows(mlp_term, local_rows)).astype(jnp.bfloat16)
    cot_rows = collect_rows(out_cotangent)
    gain_two, bias_two, gate_up_local, down_local = mlp_params(
        norm2_gain, norm2_bias, gate_up_weight, down_weight
    )
    grad_act = lax.dot_general(
        cot_rows, down_local, (((1,), (1,)), ((), ())), preferred_element_type=jnp.float32
    )
    grad_gate = (
        grad_act * up_proj * sigmoid_gate * (1.0 + gate_proj * (1.0 - sigmoid_gate))
    ).astype(jnp.bfloat16)
    grad_up = (grad_act * silu_gate).astype(jnp.bfloat16)
    grad_down = lax.dot_general(
        activation, cot_rows, (((0,), (0,)), ((), ())), preferred_element_type=jnp.float32
    )
    grad_wgate = lax.dot_general(
        rows_two, grad_gate, (((0,), (0,)), ((), ())), preferred_element_type=jnp.float32
    )
    grad_wup = lax.dot_general(
        rows_two, grad_up, (((0,), (0,)), ((), ())), preferred_element_type=jnp.float32
    )

    def mlp_back_term(row_start, row_count):
        gate_back = lax.dot_general(
            grad_gate,
            gate_up_local[0],
            (((1,), (1,)), ((), ())),
            preferred_element_type=jnp.float32,
        )
        up_back = lax.dot_general(
            grad_up, gate_up_local[1], (((1,), (1,)), ((), ())), preferred_element_type=jnp.float32
        )
        return gate_back + up_back

    grad_normed_two = spread_rows(mlp_back_term, local_rows)
    grad_gain_two = jnp.sum(grad_normed_two * hat_two, axis=0)
    grad_bias_two = jnp.sum(grad_normed_two, axis=0)
    grad_resid = out_cotangent.astype(jnp.float32) + norm_back(
        grad_normed_two * gain_two.astype(jnp.float32), hat_two, inv_two
    )
    mlp_shares = (
        lax.psum_scatter(
            grad_wgate.astype(jnp.bfloat16), "dp", scatter_dimension=0, tiled=True
        ).astype(jnp.float32),
        lax.psum_scatter(
            grad_wup.astype(jnp.bfloat16), "dp", scatter_dimension=0, tiled=True
        ).astype(jnp.float32),
        lax.psum_scatter(
            grad_down.astype(jnp.bfloat16), "dp", scatter_dimension=1, tiled=True
        ).astype(jnp.float32),
        lax.psum_scatter(
            grad_gain_two.astype(jnp.bfloat16), "dp", scatter_dimension=0, tiled=True
        ).astype(jnp.float32),
        lax.psum_scatter(
            grad_bias_two.astype(jnp.bfloat16), "dp", scatter_dimension=0, tiled=True
        ).astype(jnp.float32),
    )
    grad_resid_rows = collect_rows(grad_resid.astype(jnp.bfloat16))
    gain_one, bias_one, qkv_local, bias_local, out_local = attention_params(
        norm1_gain, norm1_bias, qkv_weight, qkv_bias, out_weight
    )
    grad_context = lax.dot_general(
        grad_resid_rows, out_local, (((1,), (1,)), ((), ())), preferred_element_type=jnp.float32
    ).astype(jnp.bfloat16)
    grad_wout = lax.dot_general(
        context_rows, grad_resid_rows, (((0,), (0,)), ((), ())), preferred_element_type=jnp.float32
    )
    grad_ctx_heads = grad_context.reshape(seq_count, SEQ_LEN, heads_here, HEAD_DIM)

    def attend_back(pieces):
        query_seq, key_seq, value_seq, context_seq, grad_ctx_seq, total_seq = pieces
        scores = (
            jnp.einsum("qhd,khd->hqk", query_seq, key_seq, preferred_element_type=jnp.float32)
            * score_scale
        )
        scores = jnp.where(causal, scores, -jnp.inf)
        prob_full = jnp.exp(scores - total_seq[..., None])
        prob_low = prob_full.astype(jnp.bfloat16)
        grad_probs = jnp.einsum(
            "qhd,khd->hqk", grad_ctx_seq, value_seq, preferred_element_type=jnp.float32
        )
        delta_sum = jnp.einsum(
            "qhd,qhd->hq", grad_ctx_seq, context_seq, preferred_element_type=jnp.float32
        )
        grad_scores = (prob_full * (grad_probs - delta_sum[..., None]) * score_scale).astype(
            jnp.bfloat16
        )
        grad_value_seq = jnp.einsum(
            "hqk,qhd->khd", prob_low, grad_ctx_seq, preferred_element_type=jnp.float32
        )
        grad_query_seq = jnp.einsum(
            "hqk,khd->qhd", grad_scores, key_seq, preferred_element_type=jnp.float32
        )
        grad_key_seq = jnp.einsum(
            "hqk,qhd->khd", grad_scores, query_seq, preferred_element_type=jnp.float32
        )
        return (grad_query_seq, grad_key_seq, grad_value_seq)

    grad_query, grad_keys, grad_values = lax.map(
        attend_back, (query_rot, key_rot, value_heads, context, grad_ctx_heads, log_totals)
    )
    grad_query = unrotate(grad_query, cosine_table, sine_table, ROT)
    grad_keys = unrotate(grad_keys, cosine_table, sine_table, ROT)
    grad_pre = (
        jnp.stack([grad_query, grad_keys, grad_values])
        .astype(jnp.bfloat16)
        .reshape(3, group_rows, head_cols)
    )
    grad_bqkv = jnp.sum(grad_pre, axis=1, dtype=jnp.float32)
    grad_wqkv = jnp.einsum("rd,crk->cdk", rows_one, grad_pre, preferred_element_type=jnp.float32)

    def qkv_back_term(row_start, row_count):
        return jnp.einsum("crk,cdk->rd", grad_pre, qkv_local, preferred_element_type=jnp.float32)

    grad_normed_one = spread_rows(qkv_back_term, local_rows)
    grad_gain_one = jnp.sum(grad_normed_one * hat_one, axis=0)
    grad_bias_one = jnp.sum(grad_normed_one, axis=0)
    grad_input = grad_resid + norm_back(
        grad_normed_one * gain_one.astype(jnp.float32), hat_one, inv_one
    )
    attn_shares = (
        lax.psum_scatter(
            grad_wqkv.astype(jnp.bfloat16), "dp", scatter_dimension=1, tiled=True
        ).astype(jnp.float32),
        lax.psum_scatter(
            grad_bqkv.astype(jnp.bfloat16), "dp", scatter_dimension=1, tiled=True
        ).astype(jnp.float32),
        lax.psum_scatter(
            grad_wout.astype(jnp.bfloat16), "dp", scatter_dimension=1, tiled=True
        ).astype(jnp.float32),
        lax.psum_scatter(
            grad_gain_one.astype(jnp.bfloat16), "dp", scatter_dimension=0, tiled=True
        ).astype(jnp.float32),
        lax.psum_scatter(
            grad_bias_one.astype(jnp.bfloat16), "dp", scatter_dimension=0, tiled=True
        ).astype(jnp.float32),
    )
    norm_totals = lax.psum((attn_shares[3], attn_shares[4], mlp_shares[3], mlp_shares[4]), "tensor")
    grad_gate_up = jnp.stack([mlp_shares[0], mlp_shares[1]])
    return (
        layer_output,
        grad_input,
        norm_totals[0],
        norm_totals[1],
        attn_shares[0],
        attn_shares[1],
        attn_shares[2],
        norm_totals[2],
        norm_totals[3],
        grad_gate_up,
        mlp_shares[2],
    )


def solution(mesh):
    placed = (
        P(("dp", "tensor"), None),
        P("dp"),
        P("dp"),
        P(None, "dp", "tensor"),
        P(None, ("tensor", "dp")),
        P("tensor", "dp"),
        P("dp"),
        P("dp"),
        P(None, "dp", "tensor"),
        P("tensor", "dp"),
        P(("dp", "tensor"), None),
    )
    return jax.shard_map(
        shards,
        mesh=mesh,
        in_specs=placed,
        out_specs=(
            P(("dp", "tensor"), None),
            P(("dp", "tensor"), None),
            P("dp"),
            P("dp"),
            P(None, "dp", "tensor"),
            P(None, ("tensor", "dp")),
            P("tensor", "dp"),
            P("dp"),
            P("dp"),
            P(None, "dp", "tensor"),
            P("tensor", "dp"),
        ),
        check_vma=False,
    )
```

profile of v0, /device:TPU:0, one launch (start us, length us, event | category | flops | bytes accessed | tf_op | source)
XLA Modules:
  0.0 1152.0 jit_solution(1779346989243993215)
XLA Ops:
  11.1 13.5 %all-gather = bf16[8,1,256]{2,1,0:T(2,128)(2,1)S(1)} all-gather(bf16[1,1,256]{2,1,0:T(2,128)(2,1)S(1)} %reshape.169), channel_id=1, replica_groups=mesh['dp'=8,'tensor'=4] {'dp'}, dimensions={0}, use_global_device_ids=true | all-gather | bytes 4608 | tf_op jit(solution)/shard_map/all_gather | solution.py:69
  25.3 8.7 all-gather.1
  37.1 10.1 all-gather.2
  47.4 40.1 %all-gather.14.cloned.1.call-done = bf16[1024,2048]{1,0:T(8,128)(2,1)} async-done(((bf16[256,2048]{1,0:T(8,128)(2,1)}), bf16[1024,2048]{1,0:T(8,128)(2,1)}) %all-gather.14.cloned.1.call-update) | async-done | bytes 4194320 | tf_op jit(solution)/shard_map/all_gather | solution.py:87
  87.6 66.3 %all-gather.16.cloned.1.call-done = bf16[3,2048,512]{2,1,0:T(8,128)(2,1)} async-done(((bf16[3,256,512]{2,1,0:T(8,128)(2,1)}), bf16[3,2048,512]{2,1,0:T(8,128)(2,1)}) %all-gather.16.cloned.1.call-update) | async-done | bytes 6291472 | tf_op jit(solution)/shard_map/all_gather | solution.py:71
  153.9 10.2 add_bitcast_fusion
  164.1 2.4 fusion.92
  169.6 2.8 squeeze.43
  174.3 2.8 squeeze.44
  182.8 2.8 pad_maximum_fusion
  186.0 3.9 reshape.199
  189.9 3.3 copy.105
  193.2 13.7 %while.28 = (s32[]{:T(128)}, bf16[2,512,8,64]{1,3,2,0:T(8,128)(2,1)}, f32[2,8,512]{2,1,0:T(8,128)S(1)}, bf16[2,512,8,64]{1,3,2,0:T(8,128)(2,1)}, bf16[2,512,8,64...) while((s32[]{:T(128)}, bf16[2,512,8,64]{1,3,2,0:T(8,128)(2,1)}, ...), condition=%wide.region_5.6_spmd.clone, body=%wide.region_2.5_spmd.clone.sunk | while | flops 560459776 | bytes 41027748 | solution.py:153
  197.0 2.3 fusion.138
  203.6 2.3 fusion.138
  210.5 6.3 convolution_convert_fusion.4
  217.5 9.2 all-gather.3
  226.7 9.7 all-gather.4
  236.4 31.8 %reduce-scatter.13.cloned.1.call-done = bf16[256,2048]{1,0:T(8,128)(2,1)} async-done(((bf16[1024,2048]{1,0:T(8,128)(2,1)}), bf16[256,2048]{1,0:T(8,128)(2,1)}) %reduce-scatter.13.cloned.1.call-update) | async-done | bytes 1048592 | tf_op jit(solution)/shard_map/reduce_scatter | solution.py:91
  274.7 103.0 %all-gather.22.cloned.1.call-done = bf16[2,2048,1408]{2,1,0:T(8,128)(2,1)} async-done(((bf16[2,256,1408]{2,1,0:T(8,128)(2,1)}), bf16[2,2048,1408]{2,1,0:T(8,128)(2,1)}) %all-gather.22.cloned.1.call-update) | async-done | bytes 11534352 | tf_op jit(solution)/shard_map/all_gather | solution.py:81
  377.7 53.1 %all-gather.20.cloned.1.call-done = bf16[1024,2048]{1,0:T(8,128)(2,1)} async-done(((bf16[256,2048]{1,0:T(8,128)(2,1)}), bf16[1024,2048]{1,0:T(8,128)(2,1)}) %all-gather.20.cloned.1.call-update) | async-done | bytes 4194320 | tf_op jit(solution)/shard_map/all_gather | solution.py:87
  430.9 12.2 %fusion.57 = f32[1024,1408]{1,0:T(8,128)} fusion(bf16[1024,2048]{1,0:T(8,128)(2,1)} %all-gather.20.cloned.1.call-done, bf16[2,2048,1408]{2,1,0:T(8,128)(2,1)} %all-gather.22.cloned.1.call-done), kind=kOutput, calls=%fused_computation.78 | convolution fusion | flops 5905580032 | bytes 15728640 | tf_op jit(solution)/shard_map/dot_general | solution.py:168
  443.1 8.4 fusion.59
  451.5 33.8 %all-gather.26.cloned.1.call-done = bf16[1024,2048]{1,0:T(8,128)(2,1)} async-done(((bf16[256,2048]{1,0:T(8,128)(2,1)}), bf16[1024,2048]{1,0:T(8,128)(2,1)}) %all-gather.26.cloned.1.call-update) | async-done | bytes 4194320 | tf_op jit(solution)/shard_map/all_gather | solution.py:87
  485.3 62.4 %all-gather.24.cloned.1.call-done = bf16[1408,2048]{1,0:T(8,128)(2,1)} async-done(((bf16[1408,256]{1,0:T(8,128)(2,1)}), bf16[1408,2048]{1,0:T(8,128)(2,1)}) %all-gather.24.cloned.1.call-update) | async-done | bytes 5767184 | tf_op jit(solution)/shard_map/all_gather | solution.py:82
  547.8 16.7 %multiply_convert_fusion.1 = (bf16[1024,1408]{1,0:T(8,128)(2,1)}, bf16[1024,1408]{1,0:T(8,128)(2,1)}, bf16[1024,1408]{1,0:T(8,128)(2,1)}) fusion(f32[1024,1408]{1,0:T(8,128)} %fusion.57, f32[1024,1408]{1,0:T(8,128)} %fusion.59, bf16[1024,2048]{1,0:T(8,128)(2,1)} %all-gather.26.cloned.1.call-done, bf16[1408,2048]{1,0:T(8,128)(2,1)} %all-gather.24.cloned.1.call-done), kind=kOutput, calls=%fused_computation.72 | convolution fusion | flops 5927206912 | bytes 30146560 | tf_op jit(solution)/shard_map/dot_general | solution.py:182
  564.4 9.7 fusion.56
  574.2 10.2 add_convert_fusion
  584.8 50.5 %reduce-scatter.17.cloned.1.call-done = bf16[256,2048]{1,0:T(8,128)(2,1)} async-done(((bf16[1024,2048]{1,0:T(8,128)(2,1)}), bf16[256,2048]{1,0:T(8,128)(2,1)}) %reduce-scatter.17.cloned.1.call-update) | async-done | bytes 1048592 | tf_op jit(solution)/shard_map/reduce_scatter | solution.py:91
  635.4 3.3 fusion.85
  641.0 10.5 convolution_convert_fusion
  651.6 11.0 convolution_convert_fusion.2
  662.7 11.0 convolution_convert_fusion.1
  673.7 20.0 %all-gather.28.cloned.1.call-done = bf16[1024,2048]{1,0:T(8,128)(2,1)} async-done(((bf16[256,2048]{1,0:T(8,128)(2,1)}), bf16[1024,2048]{1,0:T(8,128)(2,1)}) %all-gather.28.cloned.1.call-update) | async-done | bytes 4194320 | tf_op jit(solution)/shard_map/all_gather | solution.py:87
  693.7 5.2 convolution_convert_fusion.6
  701.2 3.6 copy.112
  704.8 44.3 %while.29 = (s32[]{:T(128)}, f32[2,512,8,64]{1,3,2,0:T(8,128)}, f32[2,512,8,64]{1,3,2,0:T(8,128)}, bf16[2,512,8,64]{1,3,2,0:T(8,128)(2,1)}, bf16[2,512,8,64]{1,3...) while((s32[]{:T(128)}, f32[2,512,8,64]{1,3,2,0:T(8,128)}, ...), condition=%wide.region_14.15_spmd.clone, body=%wide.region_13.14_spmd.clone.sunk | while | flops 1366552576 | bytes 111810008 | solution.py:275
  712.5 2.6 fusion.149
  715.3 3.5 multiply_convert_fusion.5
  723.7 3.2 fusion.152
  734.6 2.7 fusion.149
  737.4 3.5 multiply_convert_fusion.5
  745.9 3.2 fusion.152
  749.1 3.4 copy.120
  762.8 2.6 copy.142
  767.5 2.7 copy.144
  772.2 2.4 constant_dynamic-update-slice_fusion.2
  776.7 2.4 reduce_sum.145
  780.0 5.9 convolution_convert_fusion.5
  786.0 11.2 bitcast_convert_fusion.1
  797.2 11.0 convolution_convert_fusion.3
  808.3 11.6 %convert_bitcast_fusion = bf16[3,2048,512]{1,2,0:T(8,128)(2,1)} fusion(bf16[3,1024,512]{2,1,0:T(8,128)(2,1)} %constant_dynamic-update-slice_fusion, bf16[1024,2048]{1,0:T(8,128)(2,1)} %all-gather.14.cloned.1.call-done), kind=kOutput, calls=%fused_computation.68 | convolution fusion | flops 6445596672 | bytes 13631488 | tf_op jit(solution)/shard_map/rd,crk->cdk/dot_general | solution.py:286
  822.0 2.3 convert_element_type.187
  826.2 65.6 %reduce-scatter.27.cloned.1.call-done = bf16[256,1408]{1,0:T(8,128)(2,1)} async-done(((bf16[2048,1408]{1,0:T(8,128)(2,1)}), bf16[256,1408]{1,0:T(8,128)(2,1)}) %reduce-scatter.27.cloned.1.call-update) | async-done | bytes 720912 | tf_op jit(solution)/shard_map/reduce_scatter | solution.py:221
  891.8 3.2 maximum_convert_fusion
  895.0 28.5 %reduce-scatter.31.cloned.1.call-done = bf16[64,3]{1,0:T(8,128)(2,1)} async-done(((bf16[512,3]{1,0:T(8,128)(2,1)}), bf16[64,3]{1,0:T(8,128)(2,1)}) %reduce-scatter.31.cloned.1.call-update) | async-done | bytes 400
  924.9 35.7 %reduce-scatter.23.cloned.1.call-done = bf16[512,256]{1,0:T(8,128)(2,1)} async-done(((bf16[512,2048]{1,0:T(8,128)(2,1)}), bf16[512,256]{1,0:T(8,128)(2,1)}) %reduce-scatter.23.cloned.1.call-update) | async-done | bytes 262160 | tf_op jit(solution)/shard_map/reduce_scatter | solution.py:304
  962.4 52.2 %reduce-scatter.19.cloned.1.call-done = bf16[256,2048]{1,0:T(8,128)(2,1)} async-done(((bf16[1024,2048]{1,0:T(8,128)(2,1)}), bf16[256,2048]{1,0:T(8,128)(2,1)}) %reduce-scatter.19.cloned.1.call-update) | async-done | bytes 1048592 | tf_op jit(solution)/shard_map/reduce_scatter | solution.py:91
  1018.2 28.4 %all-reduce.5 = (bf16[2048]{0:T(1024)(128)(2,1)S(1)}, bf16[2048]{0:T(1024)(128)(2,1)S(1)}, bf16[2048]{0:T(1024)(128)(2,1)S(1)}, bf16[2048]{0:T(1024)(128)(2,1)S(1)}) all-reduce(bf16[2048]{0:T(1024)(128)(2,1)S(1)} %get-tuple-element.259, bf16[2048]{0:T(1024)(128)(2,1)S(1)} %reduce_sum.144, ...), channel_id=6, replica_groups=mesh['dp'=8,'tensor'=4] {'dp'}, use_global_device_ids=true, to_apply=%region_19.20.clone | all-reduce | flops 8192 | bytes 32768
  1046.9 9.5 all-reduce.4
  1056.4 13.8 %reduce-scatter.15.cloned.1.call-done = bf16[256,2048]{1,0:T(8,128)(2,1)} async-done(((bf16[1024,2048]{1,0:T(8,128)(2,1)}), bf16[256,2048]{1,0:T(8,128)(2,1)}) %reduce-scatter.15.cloned.1.call-update) | async-done | bytes 1048592 | tf_op jit(solution)/shard_map/reduce_scatter | solution.py:91
  1070.2 4.7 fusion.79
  1075.0 67.2 %reduce-scatter.21.cloned.1.call-done = bf16[3,256,512]{1,2,0:T(8,128)(2,1)} async-done(((bf16[3,2048,512]{1,2,0:T(8,128)(2,1)}), bf16[3,256,512]{1,2,0:T(8,128)(2,1)}) %reduce-scatter.21.cloned.1.call-update) | async-done | bytes 786448 | tf_op jit(solution)/shard_map/reduce_scatter | solution.py:298
  1142.1 2.6 copy.130
  (281 shorter events, 96.6 us)
Async XLA Ops:
  7.2 26.9 %copy-start = (bf16[256,2048]{1,0:T(8,128)(2,1)S(1)}, bf16[256,2048]{1,0:T(8,128)(2,1)}, u32[]{:S(2)}) copy-start(bf16[256,2048]{1,0:T(8,128)(2,1)} %param.15) | copy-start | bytes 3145732
  7.2 80.4 %all-gather.14.cloned.1.call-start = ((), (), s32[]{:S(2)}) async-start(), calls=%async_computation.10 | async-start | bytes 5242880 | tf_op jit(solution)/shard_map/all_gather | solution.py:87
  8.8 28.3 %copy-start.47 = (bf16[3,64]{1,0:T(4,128)(2,1)S(1)}, bf16[3,64]{1,0:T(4,128)(2,1)}, u32[]{:S(2)}) copy-start(bf16[3,64]{1,0:T(4,128)(2,1)} %param.19) | copy-start | bytes 1156
  8.8 25.2 %copy-start.36 = (f32[256]{0:T(256)}, f32[256]{0:T(256)S(1)}, u32[]{:S(2)}) copy-start(f32[256]{0:T(256)S(1)} %broadcast_multiply_fusion.5) | copy-start | bytes 3076
  10.4 23.6 %copy-start.41 = (f32[256]{0:T(256)}, f32[256]{0:T(256)S(1)}, u32[]{:S(2)}) copy-start(f32[256]{0:T(256)S(1)} %add_rsqrt_fusion.1) | copy-start | bytes 3076
  24.6 9.4 copy-start.32
  35.5 118.4 %all-gather.16.cloned.1.call-start = ((), (), s32[]{:S(2)}) async-start(), calls=%async_computation.11 | async-start | bytes 7077888 | tf_op jit(solution)/shard_map/all_gather | solution.py:71
  36.3 174.2 %all-gather.18.cloned.1.call-start = ((), (), s32[]{:S(2)}) async-start(), calls=%async_computation.12 | async-start | bytes 2359296 | tf_op jit(solution)/shard_map/all_gather | solution.py:73
  37.0 231.2 %reduce-scatter.13.cloned.1.call-start = ((), (), s32[]{:S(2)}) async-start(), calls=%async_computation.13 | async-start | bytes 5242880 | tf_op jit(solution)/shard_map/reduce_scatter | solution.py:91
  47.4 133.6 %copy-start.28 = (f32[512,8]{0,1:T(8,128)}, f32[512,8]{0,1:T(8,128)S(1)}, u32[]{:S(2)}) copy-start(f32[512,8]{0,1:T(8,128)S(1)} %get-tuple-element.326) | copy-start | bytes 49156
  47.4 133.6 %copy-start.30 = (f32[512,8]{0,1:T(8,128)}, f32[512,8]{0,1:T(8,128)S(1)}, u32[]{:S(2)}) copy-start(f32[512,8]{0,1:T(8,128)S(1)} %get-tuple-element.327) | copy-start | bytes 49156
  216.8 9.9 copy-start.51
  216.8 160.9 %all-gather.22.cloned.1.call-start = ((), (), s32[]{:S(2)}) async-start(), calls=%async_computation.15 | async-start | bytes 12976128 | tf_op jit(solution)/shard_map/all_gather | solution.py:81
  217.4 213.5 %all-gather.20.cloned.1.call-start = ((), (), s32[]{:S(2)}) async-start(), calls=%async_computation.14 | async-start | bytes 5242880 | tf_op jit(solution)/shard_map/all_gather | solution.py:87
  226.6 412.0 %copy-start.26 = (f32[8,1,256]{2,1,0:T(1,128)}, f32[8,1,256]{2,1,0:T(1,128)S(1)}, u32[]{:S(2)}) copy-start(f32[8,1,256]{2,1,0:T(1,128)S(1)} %convert_element_type.191) | copy-start | bytes 24580
  268.2 3.4 copy-start.6
  269.9 368.8 %copy-start.34 = (f32[256]{0:T(256)}, f32[256]{0:T(256)S(1)}, u32[]{:S(2)}) copy-start(f32[256]{0:T(256)S(1)} %broadcast_multiply_fusion.4) | copy-start | bytes 3076
  271.6 367.1 %copy-start.38 = (f32[256]{0:T(256)}, f32[256]{0:T(256)S(1)}, u32[]{:S(2)}) copy-start(f32[256]{0:T(256)S(1)} %add_rsqrt_fusion) | copy-start | bytes 3076
  273.2 212.1 %all-gather.26.cloned.1.call-start = ((), (), s32[]{:S(2)}) async-start(), calls=%async_computation.18 | async-start | bytes 5242880 | tf_op jit(solution)/shard_map/all_gather | solution.py:87
  273.9 273.8 %all-gather.24.cloned.1.call-start = ((), (), s32[]{:S(2)}) async-start(), calls=%async_computation.16 | async-start | bytes 6488064 | tf_op jit(solution)/shard_map/all_gather | solution.py:82
  274.7 360.6 %reduce-scatter.17.cloned.1.call-start = ((), (), s32[]{:S(2)}) async-start(), calls=%async_computation.19 | async-start | bytes 5242880 | tf_op jit(solution)/shard_map/reduce_scatter | solution.py:91
  430.9 12.3 %copy-start.48 = (bf16[2,2048,1408]{2,1,0:T(8,128)(2,1)S(1)}, bf16[2,2048,1408]{2,1,0:T(8,128)(2,1)}, u32[]{:S(2)}) copy-start(bf16[2,2048,1408]{2,1,0:T(8,128)(2,1)} %all-gather.22.cloned.1.call-done) | copy-start | bytes 34603012
  430.9 12.3 %copy-start.49 = (bf16[1024,2048]{1,0:T(8,128)(2,1)S(1)}, bf16[1024,2048]{1,0:T(8,128)(2,1)}, u32[]{:S(2)}) copy-start(bf16[1024,2048]{1,0:T(8,128)(2,1)} %all-gather.20.cloned.1.call-done) | copy-start | bytes 12582916
  547.7 26.4 %slice-start = ((s8[11534336]{0:T(1024)(128)(4,1)}), s8[3145728]{0:T(1024)(128)(4,1)S(1)}, s32[]{:S(2)}) async-start(s8[11534336]{0:T(1024)(128)(4,1)} %bitcast.203), calls=%async_computation.28 | async-start | bytes 6291456
  547.7 26.4 %slice-start.1 = ((s8[11534336]{0:T(1024)(128)(4,1)}), s8[4194304]{0:T(1024)(128)(4,1)S(1)}, s32[]{:S(2)}) async-start(s8[11534336]{0:T(1024)(128)(4,1)} %bitcast.203), calls=%async_computation.29 | async-start | bytes 8388608
  564.4 9.8 slice-start.2
  584.4 109.3 %all-gather.28.cloned.1.call-start = ((), (), s32[]{:S(2)}) async-start(), calls=%async_computation.20 | async-start | bytes 5242880 | tf_op jit(solution)/shard_map/all_gather | solution.py:87
  635.3 3.4 copy-start.7
  635.3 3.4 copy-start.9
  635.3 3.4 copy-start.14
  641.0 181.0 %reduce-scatter.29.cloned.1.call-start = ((), (), s32[]{:S(2)}) async-start(), calls=%async_computation.26 | async-start | bytes 6488064 | tf_op jit(solution)/shard_map/reduce_scatter | solution.py:224
  651.6 174.7 %reduce-scatter.25.cloned.1.call-start = ((), (), s32[]{:S(2)}) async-start(), calls=%async_computation.24 | async-start | bytes 6488064 | tf_op jit(solution)/shard_map/reduce_scatter | solution.py:218
  662.6 229.2 %reduce-scatter.27.cloned.1.call-start = ((), (), s32[]{:S(2)}) async-start(), calls=%async_computation.25 | async-start | bytes 6488064 | tf_op jit(solution)/shard_map/reduce_scatter | solution.py:221
  673.6 249.9 %reduce-scatter.31.cloned.1.call-start = ((), (), s32[]{:S(2)}) async-start(), calls=%async_computation.27 | async-start | bytes 147456
  704.8 5.2 copy-start.24
  712.5 2.8 copy-start.11
  712.5 2.8 copy-start.22
  715.3 3.5 copy-start.3
  715.3 3.5 copy-start.19
  726.9 5.2 copy-start.24
  734.6 2.7 copy-start.25
  734.6 2.8 copy-start.11
  734.6 2.8 copy-start.22
  737.4 3.5 copy-start.3
  737.4 3.5 copy-start.19
  741.8 2.7 copy-start.20
  749.1 4.9 copy-start.18
  772.2 3.5 copy-start.15
  775.7 4.3 copy-start.23
  779.9 180.7 %reduce-scatter.23.cloned.1.call-start = ((), (), s32[]{:S(2)}) async-start(), calls=%async_computation.23 | async-start | bytes 2359296 | tf_op jit(solution)/shard_map/reduce_scatter | solution.py:304
  785.9 228.7 %reduce-scatter.19.cloned.1.call-start = ((), (), s32[]{:S(2)}) async-start(), calls=%async_computation.21 | async-start | bytes 5242880 | tf_op jit(solution)/shard_map/reduce_scatter | solution.py:91
  797.2 273.0 %reduce-scatter.15.cloned.1.call-start = ((), (), s32[]{:S(2)}) async-start(), calls=%async_computation.17 | async-start | bytes 5242880 | tf_op jit(solution)/shard_map/reduce_scatter | solution.py:91
  808.2 333.9 %reduce-scatter.21.cloned.1.call-start = ((), (), s32[]{:S(2)}) async-start(), calls=%async_computation.22 | async-start | bytes 7077888 | tf_op jit(solution)/shard_map/reduce_scatter | solution.py:298
  891.8 124.2 %copy-start.1 = (bf16[256,2048]{1,0:T(8,128)(2,1)S(1)}, bf16[256,2048]{1,0:T(8,128)(2,1)}, u32[]{:S(2)}) copy-start(bf16[256,2048]{1,0:T(8,128)(2,1)} %param.15) | copy-start | bytes 3145732
  891.8 124.2 %copy-start.33 = (f32[8,1,256]{2,1,0:T(1,128)S(1)}, f32[8,1,256]{2,1,0:T(1,128)}, u32[]{:S(2)}) copy-start(f32[8,1,256]{2,1,0:T(1,128)} %copy-done.32) | copy-start | bytes 24580
  891.8 124.2 %copy-start.37 = (f32[256]{0:T(256)S(1)}, f32[256]{0:T(256)}, u32[]{:S(2)}) copy-start(f32[256]{0:T(256)} %copy-done.36) | copy-start | bytes 3076
  891.8 124.2 %copy-start.42 = (f32[256]{0:T(256)S(1)}, f32[256]{0:T(256)}, u32[]{:S(2)}) copy-start(f32[256]{0:T(256)} %copy-done.41) | copy-start | bytes 3076
  895.0 123.2 %copy-start.40 = (bf16[2048]{0:T(1024)(128)(2,1)S(1)}, bf16[2048]{0:T(1024)(128)(2,1)}, u32[]{:S(2)}) copy-start(bf16[2048]{0:T(1024)(128)(2,1)} %get-tuple-element.257) | copy-start | bytes 12292
  895.0 175.2 %copy-start.8 = (bf16[256,2048]{1,0:T(8,128)(2,1)S(1)}, bf16[256,2048]{1,0:T(8,128)(2,1)}, u32[]{:S(2)}) copy-start(bf16[256,2048]{1,0:T(8,128)(2,1)} %reduce-scatter.13.cloned.1.call-done) | copy-start | bytes 3145732
  895.0 175.2 %copy-start.27 = (f32[8,1,256]{2,1,0:T(1,128)S(1)}, f32[8,1,256]{2,1,0:T(1,128)}, u32[]{:S(2)}) copy-start(f32[8,1,256]{2,1,0:T(1,128)} %copy-done.26) | copy-start | bytes 24580
  895.0 175.2 %copy-start.35 = (f32[256]{0:T(256)S(1)}, f32[256]{0:T(256)}, u32[]{:S(2)}) copy-start(f32[256]{0:T(256)} %copy-done.34) | copy-start | bytes 3076
  895.0 175.2 %copy-start.39 = (f32[256]{0:T(256)S(1)}, f32[256]{0:T(256)}, u32[]{:S(2)}) copy-start(f32[256]{0:T(256)} %copy-done.38) | copy-start | bytes 3076
  895.0 175.2 %copy-start.44 = (f32[256]{0:T(256)S(1)}, f32[256]{0:T(256)}, u32[]{:S(2)}) copy-start(f32[256]{0:T(256)} %copy-done.43) | copy-start | bytes 3076
  895.0 175.2 %copy-start.46 = (f32[256]{0:T(256)S(1)}, f32[256]{0:T(256)}, u32[]{:S(2)}) copy-start(f32[256]{0:T(256)} %copy-done.45) | copy-start | bytes 3076
  (25 other events, 41.6 us)
Sparse Core Ops, SparseCore 0:
  35.6 51.8 all-gather.13
  89.2 64.6 all-gather.15
  155.5 29.2 all-gather.17
  216.9 51.2 reduce-scatter.12
  269.6 108.0 all-gather.21
  380.0 50.8 all-gather.19
  432.7 52.5 all-gather.25
  486.9 60.7 all-gather.23
  584.5 50.8 reduce-scatter.16
  641.1 52.5 all-gather.27
  696.0 64.7 reduce-scatter.28
  763.0 63.2 reduce-scatter.24
  828.5 63.2 reduce-scatter.26
  894.5 29.0 reduce-scatter.30
  926.3 34.3 reduce-scatter.22
  963.5 51.0 reduce-scatter.18
  1017.4 52.7 reduce-scatter.14
  1072.4 69.7 reduce-scatter.20
where the time goes:
time: 1160 us; the launch traced here: 1150 us
  waiting for transfers between devices  730 us (63%)
  matrix products  182 us (16%)
  blocking collectives  89 us (8%)
  local copies, waits for them, and re-layouts  84.5 us (7%)
  other arithmetic  49.1 us (4%)
  between operations  16.1 us (1%)
    reduce_scatter x4, waiting for transfers between devices, spread_rows(): lax.psum_scatter(term_fn(jnp.int32(0), row_total * lax.axis_size('tensor'...  148 us
    all_gather x4, waiting for transfers between devices, collect_rows(): return lax.all_gather(row_block, 'tensor', axis=0, tiled=True)  147 us
    all_gather x1, waiting for transfers between devices, mlp_params(): lax.all_gather(gate_up_weight, 'dp', axis=1, tiled=True)  103 us
    reduce_scatter x1, waiting for transfers between devices, shards(): lax.psum_scatter(grad_wqkv.astype(jnp.bfloat16), 'dp', scatter_dimension=...  67.2 us
    all_gather x1, waiting for transfers between devices, attention_params(): lax.all_gather(qkv_weight, 'dp', axis=1, tiled=True)  66.3 us
    reduce_scatter x1, waiting for transfers between devices, shards(): lax.psum_scatter(grad_wup.astype(jnp.bfloat16), 'dp', scatter_dimension=0...  65.6 us
    all_gather x1, waiting for transfers between devices, mlp_params(): lax.all_gather(down_weight, 'dp', axis=1, tiled=True)  62.4 us
    reduce_scatter x1, waiting for transfers between devices, shards(): lax.psum_scatter(grad_wout.astype(jnp.bfloat16), 'dp', scatter_dimension=...  35.7 us
  transfers between devices with their start and end apart: 18, of which 16 were waited for; matrix products, arithmetic and copies ran while one was open for 22% of the time, Pallas kernels for 0%

commit v1 on v0

--- a/solution.py
+++ b/solution.py
@@ -7,6 +7,18 @@
 ROT = 16
 SEQ_LEN = 512
 epsilon = 1e-05
+
+
+def gather_by_bits(array, axis, dim):
+    ways, here, step = (lax.axis_size(axis), lax.axis_index(axis), array.shape[dim])
+    line, have = (array, 1)
+    while have < ways:
+        line = jnp.concatenate(
+            [line, lax.ppermute(line, axis, [(d, (d - have) % ways) for d in range(ways)])],
+            axis=dim,
+        )
+        have = 2 * have
+    return jnp.roll(line, here * step, axis=dim)
 
 
 def layer_norm(values):
@@ -84,7 +96,7 @@
 
 
 def collect_rows(row_block):
-    return lax.all_gather(row_block, "tensor", axis=0, tiled=True)
+    return gather_by_bits(row_block, "tensor", 0)
 
 
 def spread_rows(term_fn, row_total):

time: 1160 us -> 982 us (0.85)
  waiting for transfers between devices: 730 us -> 492 us
  other arithmetic: 49.1 us -> 97.7 us
  starting transfers between devices: 1.13 us -> 15.3 us
    ppermute x0 -> x8, waiting for transfers between devices: none -> 206 us  [gather_by_bits(): lax.ppermute(line, axis, [(d, (d - have) % ways) for d in range(ways)])]
    all_gather x4 -> x0, waiting for transfers between devices: 147 us -> none  [collect_rows(): return lax.all_gather(row_block, 'tensor', axis=0, tiled=True)]
    all_gather x1, waiting for transfers between devices: 103 us -> 0.01 us  [mlp_params(): lax.all_gather(gate_up_weight, 'dp', axis=1, tiled=True)]
    all_gather x1, waiting for transfers between devices: 66.3 us -> 0.01 us  [attention_params(): lax.all_gather(qkv_weight, 'dp', axis=1, tiled=True)]
    reduce_scatter x1, waiting for transfers between devices: 65.6 us -> 0.02 us  [shards(): lax.psum_scatter(grad_wup.astype(jnp.bfloat16), 'dp', scatter_dimension=0...]
    concatenate x0 -> x6, other arithmetic: none -> 40.1 us  [the longest x2 34 us: gather_by_bits(): return jnp.roll(line, here * step, axis=dim)]
    all_gather x1, waiting for transfers between devices: 62.4 us -> 27.3 us  [mlp_params(): lax.all_gather(down_weight, 'dp', axis=1, tiled=True)]
    unnamed x19 -> x15, waiting for transfers between devices: 32 us -> 14 us
  transfers between devices with their start and end apart: 18 -> 22, of which waited for: 16 -> 15; matrix products, arithmetic and copies ran while one was open for 22% -> 31% of each run, Pallas kernels for 0% -> 0%
where the time goes in v1:
time: 982 us; the launch traced here: 971 us
  waiting for transfers between devices  492 us (50%)
  matrix products  175 us (18%)
  other arithmetic  97.7 us (10%)
  blocking collectives  91.7 us (9%)
  local copies, waits for them, and re-layouts  82.6 us (8%)
  between operations  15.6 us (2%)
  starting transfers between devices  15.3 us (2%)
    ppermute x8, waiting for transfers between devices, gather_by_bits(): lax.ppermute(line, axis, [(d, (d - have) % ways) for d in range(ways)])  206 us
    reduce_scatter x4, waiting for transfers between devices, spread_rows(): lax.psum_scatter(term_fn(jnp.int32(0), row_total * lax.axis_size('tensor'...  142 us
    reduce_scatter x1, waiting for transfers between devices, shards(): lax.psum_scatter(grad_wqkv.astype(jnp.bfloat16), 'dp', scatter_dimension=...  67.2 us
    reduce_scatter x1, waiting for transfers between devices, shards(): lax.psum_scatter(grad_wout.astype(jnp.bfloat16), 'dp', scatter_dimension=...  35.7 us
    concatenate x2, other arithmetic, gather_by_bits(): return jnp.roll(line, here * step, axis=dim)  34 us
    unnamed x1, blocking collectives  28.4 us
    all_gather x1, waiting for transfers between devices, mlp_params(): lax.all_gather(down_weight, 'dp', axis=1, tiled=True)  27.3 us
  transfers between devices with their start and end apart: 22, of which 15 were waited for; matrix products, arithmetic and copies ran while one was open for 31% of the time, Pallas kernels for 0%

profile of v1, /device:TPU:0, one launch (start us, length us, event | category | flops | bytes accessed | tf_op | source)
XLA Modules:
  0.0 970.9 jit_solution(367154697382319040)
XLA Ops:
  8.6 13.5 %all-gather = bf16[8,1,256]{2,1,0:T(2,128)(2,1)S(1)} all-gather(bf16[1,1,256]{2,1,0:T(2,128)(2,1)S(1)} %reshape.169), channel_id=1, replica_groups=mesh['dp'=8,'tensor'=4] {'dp'}, dimensions={0}, use_global_device_ids=true | all-gather | bytes 4608 | tf_op jit(solution)/shard_map/all_gather | solution.py:81
  22.8 9.3 all-gather.1
  36.9 2.5 collective-permute-start
  39.4 23.0 %collective-permute-done = bf16[256,2048]{1,0:T(8,128)(2,1)S(1)} collective-permute-done((bf16[256,2048]{1,0:T(8,128)(2,1)S(1)}, bf16[256,2048]{1,0:T(8,128)(2,1)S(1)}, u32[]{:S(2)}, u32[]{:S(2)}) %collective-permute-start) | collective-permute-done | bytes 1048608 | tf_op jit(solution)/shard_map/ppermute | solution.py:17
  65.4 11.4 %all-gather.2 = bf16[8,64,3]{1,2,0:T(4,128)(2,1)S(1)} all-gather(bf16[1,64,3]{1,2,0:T(4,128)(2,1)S(1)} %bitcast.199), channel_id=1, replica_groups=mesh['dp'=8,'tensor'=4] {'dp'}, dimensions={0}, use_global_device_ids=true | all-gather | bytes 3456 | tf_op jit(solution)/shard_map/all_gather | solution.py:84
  77.1 34.3 %collective-permute-done.1 = bf16[512,2048]{1,0:T(8,128)(2,1)} collective-permute-done((bf16[512,2048]{1,0:T(8,128)(2,1)}, bf16[512,2048]{1,0:T(8,128)(2,1)}, u32[]{:S(2)}, u32[]{:S(2)}) %collective-permute-start.1) | collective-permute-done | bytes 2097184 | tf_op jit(solution)/shard_map/ppermute | solution.py:17
  111.3 13.0 %fusion.78 = bf16[1024,2048,1]{1,0,2:T(8,128)(2,1)} fusion(s32[]{:T(128)S(6)} %select_n.26, bf16[256,2048]{1,0:T(8,128)(2,1)S(1)} %fusion.92, bf16[256,2048]{1,0:T(8,128)(2,1)S(1)} %collective-permute-done, bf16[512,2048]{1,0:T(8,128)(2,1)} %collective-permute-done.1), kind=kLoop, calls=%fused_computation.123 | loop fusion | flops 25165824 | bytes 8388612 | tf_op jit(solution)/shard_map/jit(_roll_dynamic)/dynamic_slice | solution.py:21
  124.3 10.2 %add_bitcast_fusion = f32[3,1024,512]{2,1,0:T(8,128)S(1)} fusion(f32[3,512]{1,0:T(4,128)S(1)} %bitcast.198, bf16[1024,2048,1]{1,0,2:T(8,128)(2,1)} %fusion.78, bf16[3,2048,512]{2,1,0:T(8,128)(2,1)} %all-gather.10.cloned.1.call-done), kind=kOutput, calls=%fused_computation.93 | convolution fusion | flops 6444023808 | bytes 16783360 | tf_op jit(solution)/shard_map/rd,cdk->crk/dot_general | solution.py:142
  134.5 2.4 fusion.108
  139.9 2.8 squeeze.43
  144.6 3.2 squeeze.44
  156.9 3.9 reshape.199
  160.8 3.3 copy.105
  164.1 11.5 %while.28 = (s32[]{:T(128)}, bf16[2,512,8,64]{1,3,2,0:T(8,128)(2,1)S(1)}, f32[2,8,512]{2,1,0:T(8,128)S(1)}, bf16[2,512,8,64]{1,3,2,0:T(8,128)(2,1)}, bf16[2,512,...) while((s32[]{:T(128)}, bf16[2,512,8,64]{1,3,2,0:T(8,128)(2,1)S(1)}, ...), condition=%wide.region_5.7_spmd.clone, body=%wide.region_2.6_spmd.clone.sunk | while | flops 560459776 | bytes 32639084 | solution.py:165
  177.9 6.4 convolution_convert_fusion.4
  184.9 3.4 collective-permute-start.4
  188.4 10.9 %all-gather.3 = bf16[8,1,256]{2,1,0:T(2,128)(2,1)S(1)} all-gather(bf16[1,1,256]{2,1,0:T(2,128)(2,1)S(1)} %reshape.175), channel_id=1, replica_groups=mesh['dp'=8,'tensor'=4] {'dp'}, dimensions={0}, use_global_device_ids=true | all-gather | bytes 4608 | tf_op jit(solution)/shard_map/all_gather | solution.py:91
  199.3 8.8 all-gather.4
  208.1 46.7 %reduce-scatter.13.cloned.1.call-done = bf16[256,2048]{1,0:T(8,128)(2,1)} async-done(((bf16[1024,2048]{1,0:T(8,128)(2,1)}), bf16[256,2048]{1,0:T(8,128)(2,1)}) %reduce-scatter.13.cloned.1.call-update) | async-done | bytes 1048592 | tf_op jit(solution)/shard_map/reduce_scatter | solution.py:103
  263.7 19.9 %collective-permute-done.2 = bf16[256,2048]{1,0:T(8,128)(2,1)S(1)} collective-permute-done((bf16[256,2048]{1,0:T(8,128)(2,1)S(1)}, bf16[256,2048]{1,0:T(8,128)(2,1)S(1)}, u32[]{:S(2)}, u32[]{:S(2)}) %collective-permute-start.2) | collective-permute-done | bytes 1048608 | tf_op jit(solution)/shard_map/ppermute | solution.py:17
  285.3 25.4 %collective-permute-done.5 = bf16[512,2048]{1,0:T(8,128)(2,1)S(1)} collective-permute-done((bf16[512,2048]{1,0:T(8,128)(2,1)S(1)}, bf16[512,2048]{1,0:T(8,128)(2,1)S(1)}, u32[]{:S(2)}, u32[]{:S(2)}) %collective-permute-start.5) | collective-permute-done | bytes 2097184 | tf_op jit(solution)/shard_map/ppermute | solution.py:17
  310.7 43.4 %collective-permute-done.3 = bf16[512,2048]{1,0:T(8,128)(2,1)S(1)} collective-permute-done((bf16[512,2048]{1,0:T(8,128)(2,1)S(1)}, bf16[512,2048]{1,0:T(8,128)(2,1)S(1)}, u32[]{:S(2)}, u32[]{:S(2)}) %collective-permute-start.3) | collective-permute-done | bytes 2097184 | tf_op jit(solution)/shard_map/ppermute | solution.py:17
  354.1 23.2 %fusion.67 = (bf16[1024,2048]{1,0:T(8,128)(2,1)}, bf16[1024,2048]{1,0:T(8,128)(2,1)}) fusion(s32[]{:T(128)S(6)} %select_n.26, bf16[256,2048]{1,0:T(8,128)(2,1)} %param.27, bf16[256,2048]{1,0:T(8,128)(2,1)} %collective-permute-done.4, bf16[512,2048]{1,0:T(8,128)(2,1)S(1)} %collective-permute-done.5, bf16[512,2048]{1,0:T(8,128)(2,1)S(1)} %collective-permute-done.3, ...), kind=kLoop, calls=%fused_computation.112 | loop fusion | flops 50331648 | bytes 16777220 | tf_op jit(solution)/shard_map/jit(_roll_dynamic)/concatenate | solution.py:21
  377.3 11.9 %fusion.57 = f32[1024,1408]{1,0:T(8,128)} fusion(bf16[1024,2048]{1,0:T(8,128)(2,1)} %get-tuple-element.330, bf16[2,2048,1408]{2,1,0:T(8,128)(2,1)} %all-gather.14.cloned.1.call-done), kind=kOutput, calls=%fused_computation.102 | convolution fusion | flops 5905580032 | bytes 15728640 | tf_op jit(solution)/shard_map/dot_general | solution.py:180
  389.2 8.4 fusion.59
  397.7 27.3 %all-gather.16.cloned.1.call-done = bf16[1408,2048]{1,0:T(8,128)(2,1)} async-done(((bf16[1408,256]{1,0:T(8,128)(2,1)}), bf16[1408,2048]{1,0:T(8,128)(2,1)}) %all-gather.16.cloned.1.call-update) | async-done | bytes 5767184 | tf_op jit(solution)/shard_map/all_gather | solution.py:94
  425.0 16.9 %multiply_convert_fusion.1 = (bf16[1024,1408]{1,0:T(8,128)(2,1)}, bf16[1024,1408]{1,0:T(8,128)(2,1)}, bf16[1024,1408]{1,0:T(8,128)(2,1)}) fusion(f32[1024,1408]{1,0:T(8,128)} %fusion.57, f32[1024,1408]{1,0:T(8,128)} %fusion.59, bf16[1024,2048]{1,0:T(8,128)(2,1)} %get-tuple-element.329, bf16[1408,2048]{1,0:T(8,128)(2,1)} %all-gather.16.cloned.1.call-done), kind=kOutput, calls=%fused_computation.96 | convolution fusion | flops 5927206912 | bytes 30146560 | tf_op jit(solution)/shard_map/dot_general | solution.py:194
  441.9 9.7 %fusion.56 = f32[1024,2048]{1,0:T(8,128)S(1)} fusion(bf16[1024,1408]{1,0:T(8,128)(2,1)} %get-tuple-element.309, bf16[2,2048,1408]{2,1,0:T(8,128)(2,1)} %all-gather.14.cloned.1.call-done), kind=kOutput, calls=%fused_computation.101 | convolution fusion | flops 5905580032 | bytes 17039360 | tf_op jit(solution)/shard_map/dot_general | solution.py:212
  451.7 10.1 %add_convert_fusion = bf16[1024,2048]{1,0:T(8,128)(2,1)} fusion(f32[1024,2048]{1,0:T(8,128)S(1)} %fusion.56, bf16[1024,1408]{1,0:T(8,128)(2,1)} %get-tuple-element.308, bf16[2,2048,1408]{2,1,0:T(8,128)(2,1)S(1)} %bitcast.201), kind=kOutput, calls=%fused_computation.88 | convolution fusion | flops 5909774336 | bytes 21233664 | tf_op jit(solution)/shard_map/dot_general | solution.py:218
  461.9 10.5 %convolution_convert_fusion = bf16[1408,2048]{1,0:T(8,128)(2,1)} fusion(bf16[1024,1408]{1,0:T(8,128)(2,1)} %get-tuple-element.310, bf16[1024,2048]{1,0:T(8,128)(2,1)} %get-tuple-element.329), kind=kOutput, calls=%fused_computation.89 | convolution fusion | flops 5908463616 | bytes 12845056 | tf_op jit(solution)/shard_map/dot_general | solution.py:201
  472.4 11.6 %convolution_convert_fusion.2 = bf16[2048,1408]{1,0:T(8,128)(2,1)} fusion(bf16[1024,2048]{1,0:T(8,128)(2,1)} %get-tuple-element.330, bf16[1024,1408]{1,0:T(8,128)(2,1)} %get-tuple-element.309), kind=kOutput, calls=%fused_computation.91 | convolution fusion | flops 5908463616 | bytes 12845056 | tf_op jit(solution)/shard_map/dot_general | solution.py:204
  484.1 28.7 %reduce-scatter.17.cloned.1.call-done = bf16[256,2048]{1,0:T(8,128)(2,1)} async-done(((bf16[1024,2048]{1,0:T(8,128)(2,1)}), bf16[256,2048]{1,0:T(8,128)(2,1)}) %reduce-scatter.17.cloned.1.call-update) | async-done | bytes 1048592 | tf_op jit(solution)/shard_map/reduce_scatter | solution.py:103
  512.8 3.0 fusion.101
  515.8 3.7 fusion.107
  520.9 8.6 convolution_convert_fusion.1
  529.6 14.8 %collective-permute-done.6 = bf16[256,2048]{1,0:T(8,128)(2,1)S(1)} collective-permute-done((bf16[256,2048]{1,0:T(8,128)(2,1)}, bf16[256,2048]{1,0:T(8,128)(2,1)S(1)}, u32[]{:S(2)}, u32[]{:S(2)}) %collective-permute-start.6) | collective-permute-done | bytes 1048608 | tf_op jit(solution)/shard_map/ppermute | solution.py:17
  544.4 2.8 pad_maximum_fusion.3
  548.7 45.2 %collective-permute-done.7 = bf16[512,2048]{1,0:T(8,128)(2,1)} collective-permute-done((bf16[512,2048]{1,0:T(8,128)(2,1)}, bf16[512,2048]{1,0:T(8,128)(2,1)}, u32[]{:S(2)}, u32[]{:S(2)}) %collective-permute-start.7) | collective-permute-done | bytes 2097184 | tf_op jit(solution)/shard_map/ppermute | solution.py:17
  593.9 10.8 %fusion.62 = bf16[1024,2048]{1,0:T(8,128)(2,1)S(1)} fusion(s32[]{:T(128)S(6)} %select_n.26, bf16[256,2048]{1,0:T(8,128)(2,1)} %fusion.107, bf16[256,2048]{1,0:T(8,128)(2,1)S(1)} %collective-permute-done.6, bf16[512,2048]{1,0:T(8,128)(2,1)} %collective-permute-done.7), kind=kLoop, calls=%fused_computation.107 | loop fusion | flops 25165824 | bytes 8388612 | tf_op jit(solution)/shard_map/jit(_roll_dynamic)/concatenate | solution.py:21
  611.2 2.5 copy.112
  613.7 42.8 %while.29 = (s32[]{:T(128)}, f32[2,512,8,64]{1,3,2,0:T(8,128)}, f32[2,512,8,64]{1,3,2,0:T(8,128)}, bf16[2,512,8,64]{1,3,2,0:T(8,128)(2,1)}, bf16[2,512,8,64]{1,3...) while((s32[]{:T(128)}, f32[2,512,8,64]{1,3,2,0:T(8,128)}, ...), condition=%wide.region_14.16_spmd.clone, body=%wide.region_13.15_spmd.clone.sunk | while | flops 1366552576 | bytes 120198680 | solution.py:287
  620.6 2.6 fusion.167
  623.4 3.5 multiply_convert_fusion.5
  631.8 2.5 fusion.170
  642.0 2.6 fusion.167
  644.8 3.5 multiply_convert_fusion.5
  653.0 2.5 fusion.170
  656.5 3.4 copy.120
  674.0 2.6 copy.144
  682.8 6.2 convolution_convert_fusion.5
  689.1 11.1 %bitcast_convert_fusion.1 = bf16[1024,2048]{1,0:T(8,128)(2,1)} fusion(bf16[3,1024,512]{2,1,0:T(8,128)(2,1)S(1)} %constant_dynamic-update-slice_fusion, bf16[3,2048,512]{2,1,0:T(8,128)(2,1)} %all-gather.10.cloned.1.call-done), kind=kOutput, calls=%fused_computation.87 | convolution fusion | flops 6444548096 | bytes 13631488 | tf_op jit(solution)/shard_map/crk,cdk->rd/dot_general | solution.py:301
  700.3 11.0 %convolution_convert_fusion.3 = bf16[1024,2048]{1,0:T(8,128)(2,1)} fusion(bf16[1024,1408]{1,0:T(8,128)(2,1)} %get-tuple-element.310, bf16[1408,2048]{1,0:T(8,128)(2,1)} %all-gather.16.cloned.1.call-done), kind=kOutput, calls=%fused_computation.126 | convolution fusion | flops 5907677184 | bytes 12845056 | tf_op jit(solution)/shard_map/dot_general | solution.py:187
  711.4 11.0 %convert_bitcast_fusion = bf16[3,2048,512]{1,2,0:T(8,128)(2,1)} fusion(bf16[3,1024,512]{2,1,0:T(8,128)(2,1)S(1)} %constant_dynamic-update-slice_fusion, bf16[1024,2048,1]{1,0,2:T(8,128)(2,1)} %fusion.78), kind=kOutput, calls=%fused_computation.92 | convolution fusion | flops 6445596672 | bytes 13631488 | tf_op jit(solution)/shard_map/rd,crk->cdk/dot_general | solution.py:298
  724.6 2.4 convert_element_type.187
  727.1 3.2 maximum_convert_fusion
  730.2 12.6 %reduce-scatter.31.cloned.1.call-done = bf16[64,3]{1,0:T(8,128)(2,1)} async-done(((bf16[512,3]{1,0:T(8,128)(2,1)}), bf16[64,3]{1,0:T(8,128)(2,1)}) %reduce-scatter.31.cloned.1.call-update) | async-done | bytes 400
  744.2 35.7 %reduce-scatter.23.cloned.1.call-done = bf16[512,256]{1,0:T(8,128)(2,1)} async-done(((bf16[512,2048]{1,0:T(8,128)(2,1)}), bf16[512,256]{1,0:T(8,128)(2,1)}) %reduce-scatter.23.cloned.1.call-update) | async-done | bytes 262160 | tf_op jit(solution)/shard_map/reduce_scatter | solution.py:316
  781.6 52.3 %reduce-scatter.19.cloned.1.call-done = bf16[256,2048]{1,0:T(8,128)(2,1)} async-done(((bf16[1024,2048]{1,0:T(8,128)(2,1)}), bf16[256,2048]{1,0:T(8,128)(2,1)}) %reduce-scatter.19.cloned.1.call-update) | async-done | bytes 1048592 | tf_op jit(solution)/shard_map/reduce_scatter | solution.py:103
  837.5 28.4 %all-reduce.5 = (bf16[2048]{0:T(1024)(128)(2,1)S(1)}, bf16[2048]{0:T(1024)(128)(2,1)S(1)}, bf16[2048]{0:T(1024)(128)(2,1)S(1)}, bf16[2048]{0:T(1024)(128)(2,1)S(1)}) all-reduce(bf16[2048]{0:T(1024)(128)(2,1)S(1)} %get-tuple-element.260, bf16[2048]{0:T(1024)(128)(2,1)S(1)} %reduce_sum.144, ...), channel_id=6, replica_groups=mesh['dp'=8,'tensor'=4] {'dp'}, use_global_device_ids=true, to_apply=%region_19.21.clone | all-reduce | flops 8192 | bytes 32768
  866.2 9.5 all-reduce.4
  875.7 14.0 %reduce-scatter.15.cloned.1.call-done = bf16[256,2048]{1,0:T(8,128)(2,1)} async-done(((bf16[1024,2048]{1,0:T(8,128)(2,1)}), bf16[256,2048]{1,0:T(8,128)(2,1)}) %reduce-scatter.15.cloned.1.call-update) | async-done | bytes 1048592 | tf_op jit(solution)/shard_map/reduce_scatter | solution.py:103
  889.7 4.7 fusion.95
  894.4 67.2 %reduce-scatter.21.cloned.1.call-done = bf16[3,256,512]{1,2,0:T(8,128)(2,1)} async-done(((bf16[3,2048,512]{1,2,0:T(8,128)(2,1)}), bf16[3,256,512]{1,2,0:T(8,128)(2,1)}) %reduce-scatter.21.cloned.1.call-update) | async-done | bytes 786448 | tf_op jit(solution)/shard_map/reduce_scatter | solution.py:310
  961.6 2.6 copy.130
  (297 shorter events, 112.3 us)
Async XLA Ops:
  7.2 117.1 %all-gather.10.cloned.1.call-start = ((), (), s32[]{:S(2)}) async-start(), calls=%async_computation.10 | async-start | bytes 7077888 | tf_op jit(solution)/shard_map/all_gather | solution.py:83
  7.9 170.0 %all-gather.12.cloned.1.call-start = ((), (), s32[]{:S(2)}) async-start(), calls=%async_computation.11 | async-start | bytes 2359296 | tf_op jit(solution)/shard_map/all_gather | solution.py:85
  22.1 14.8 %copy-start.33 = (f32[8,1,256]{2,1,0:T(1,128)}, f32[8,1,256]{2,1,0:T(1,128)S(1)}, u32[]{:S(2)}) copy-start(f32[8,1,256]{2,1,0:T(1,128)S(1)} %convert_element_type.188) | copy-start | bytes 24580
  32.0 33.3 %copy-start.48 = (bf16[3,64]{1,0:T(4,128)(2,1)S(1)}, bf16[3,64]{1,0:T(4,128)(2,1)}, u32[]{:S(2)}) copy-start(bf16[3,64]{1,0:T(4,128)(2,1)} %param.21) | copy-start | bytes 1156
  33.5 5.9 copy-start.37
  35.2 4.2 copy-start.42
  36.9 25.5 %collective-permute-start = (bf16[256,2048]{1,0:T(8,128)(2,1)S(1)}, bf16[256,2048]{1,0:T(8,128)(2,1)S(1)}, u32[]{:S(2)}, u32[]{:S(2)}) collective-permute-start(bf16[256,2048]{1,0:T(8,128)(2,1)S(1)} %fusion.92), channel_id=1, source_target_pairs={{0,3},{1,0},{2,1},{3,2},{4,7},{5,4},{6,5},{7,6},{8,11},{9,8},{10,9... | collective-permute-start | bytes 3145736 | tf_op jit(solution)/shard_map/ppermute | solution.py:17
  63.8 47.5 %collective-permute-start.1 = (bf16[512,2048]{1,0:T(8,128)(2,1)}, bf16[512,2048]{1,0:T(8,128)(2,1)}, u32[]{:S(2)}, u32[]{:S(2)}) collective-permute-start(bf16[512,2048]{1,0:T(8,128)(2,1)} %pad_maximum_fusion), channel_id=1, source_target_pairs={{0,2},{1,3},{2,0},{3,1},{4,6},{5,7},{6,4},{7,5},{8,10},{9,11},{10,... | collective-permute-start | bytes 6291464 | tf_op jit(solution)/shard_map/ppermute | solution.py:17
  65.3 189.6 %reduce-scatter.13.cloned.1.call-start = ((), (), s32[]{:S(2)}) async-start(), calls=%async_computation.12 | async-start | bytes 5242880 | tf_op jit(solution)/shard_map/reduce_scatter | solution.py:103
  77.0 74.8 %copy-start.29 = (f32[512,8]{0,1:T(8,128)}, f32[512,8]{0,1:T(8,128)S(1)}, u32[]{:S(2)}) copy-start(f32[512,8]{0,1:T(8,128)S(1)} %get-tuple-element.327) | copy-start | bytes 49156
  77.0 74.8 %copy-start.31 = (f32[512,8]{0,1:T(8,128)}, f32[512,8]{0,1:T(8,128)S(1)}, u32[]{:S(2)}) copy-start(f32[512,8]{0,1:T(8,128)S(1)} %get-tuple-element.328) | copy-start | bytes 49156
  175.6 8.7 copy-start.11
  184.3 4.1 copy-start.51
  184.3 15.0 %copy-start.52 = (bf16[256]{0:T(256)(128)(2,1)S(1)}, bf16[256]{0:T(256)(128)(2,1)}, u32[]{:S(2)}) copy-start(bf16[256]{0:T(256)(128)(2,1)} %param.24) | copy-start | bytes 1540
  184.3 70.6 %copy-start = (bf16[256,2048]{1,0:T(8,128)(2,1)S(1)}, bf16[256,2048]{1,0:T(8,128)(2,1)}, u32[]{:S(2)}) copy-start(bf16[256,2048]{1,0:T(8,128)(2,1)} %param.17) | copy-start | bytes 3145732
  184.3 193.0 %all-gather.14.cloned.1.call-start = ((), (), s32[]{:S(2)}) async-start(), calls=%async_computation.13 | async-start | bytes 12976128 | tf_op jit(solution)/shard_map/all_gather | solution.py:93
  184.9 240.1 %all-gather.16.cloned.1.call-start = ((), (), s32[]{:S(2)}) async-start(), calls=%async_computation.14 | async-start | bytes 6488064 | tf_op jit(solution)/shard_map/all_gather | solution.py:94
  184.9 75.4 %collective-permute-start.4 = (bf16[256,2048]{1,0:T(8,128)(2,1)}, bf16[256,2048]{1,0:T(8,128)(2,1)}, u32[]{:S(2)}, u32[]{:S(2)}) collective-permute-start(bf16[256,2048]{1,0:T(8,128)(2,1)} %param.27), channel_id=1, source_target_pairs={{0,3},{1,0},{2,1},{3,2},{4,7},{5,4},{6,5},{7,6},{8,11},{9,8},{10,9... | collective-permute-start | bytes 3145736 | tf_op jit(solution)/shard_map/ppermute | solution.py:17
  188.3 324.4 %reduce-scatter.17.cloned.1.call-start = ((), (), s32[]{:S(2)}) async-start(), calls=%async_computation.16 | async-start | bytes 5242880 | tf_op jit(solution)/shard_map/reduce_scatter | solution.py:103
  199.3 316.5 %copy-start.27 = (f32[8,1,256]{2,1,0:T(1,128)}, f32[8,1,256]{2,1,0:T(1,128)S(1)}, u32[]{:S(2)}) copy-start(f32[8,1,256]{2,1,0:T(1,128)S(1)} %convert_element_type.191) | copy-start | bytes 24580
  256.5 259.3 %copy-start.35 = (f32[256]{0:T(256)}, f32[256]{0:T(256)S(1)}, u32[]{:S(2)}) copy-start(f32[256]{0:T(256)S(1)} %broadcast_multiply_fusion.4) | copy-start | bytes 3076
  258.3 257.5 %copy-start.39 = (f32[256]{0:T(256)}, f32[256]{0:T(256)S(1)}, u32[]{:S(2)}) copy-start(f32[256]{0:T(256)S(1)} %add_rsqrt_fusion) | copy-start | bytes 3076
  258.8 24.8 %collective-permute-start.2 = (bf16[256,2048]{1,0:T(8,128)(2,1)S(1)}, bf16[256,2048]{1,0:T(8,128)(2,1)S(1)}, u32[]{:S(2)}, u32[]{:S(2)}) collective-permute-start(bf16[256,2048]{1,0:T(8,128)(2,1)S(1)} %add_convert_fusion.2), channel_id=1, source_target_pairs={{0,3},{1,0},{2,1},{3,2},{4,7},{5,4},{6,5},{7,6},{8,11},{9,8},{10,9... | collective-permute-start | bytes 3145736 | tf_op jit(solution)/shard_map/ppermute | solution.py:17
  262.2 48.6 %collective-permute-start.5 = (bf16[512,2048]{1,0:T(8,128)(2,1)S(1)}, bf16[512,2048]{1,0:T(8,128)(2,1)S(1)}, u32[]{:S(2)}, u32[]{:S(2)}) collective-permute-start(bf16[512,2048]{1,0:T(8,128)(2,1)S(1)} %pad_maximum_fusion.2), channel_id=1, source_target_pairs={{0,2},{1,3},{2,0},{3,1},{4,6},{5,7},{6,4},{7,5},{8,10},{9,11},{10,... | collective-permute-start | bytes 6291464 | tf_op jit(solution)/shard_map/ppermute | solution.py:17
  283.8 70.3 %collective-permute-start.3 = (bf16[512,2048]{1,0:T(8,128)(2,1)S(1)}, bf16[512,2048]{1,0:T(8,128)(2,1)S(1)}, u32[]{:S(2)}, u32[]{:S(2)}) collective-permute-start(bf16[512,2048]{1,0:T(8,128)(2,1)S(1)} %pad_maximum_fusion.1), channel_id=1, source_target_pairs={{0,2},{1,3},{2,0},{3,1},{4,6},{5,7},{6,4},{7,5},{8,10},{9,11},{10,... | collective-permute-start | bytes 6291464 | tf_op jit(solution)/shard_map/ppermute | solution.py:17
  377.3 11.9 %copy-start.12 = (bf16[1024,2048]{1,0:T(8,128)(2,1)S(1)}, bf16[1024,2048]{1,0:T(8,128)(2,1)}, u32[]{:S(2)}) copy-start(bf16[1024,2048]{1,0:T(8,128)(2,1)} %get-tuple-element.330) | copy-start | bytes 12582916
  377.3 11.9 %copy-start.49 = (bf16[2,2048,1408]{2,1,0:T(8,128)(2,1)S(1)}, bf16[2,2048,1408]{2,1,0:T(8,128)(2,1)}, u32[]{:S(2)}) copy-start(bf16[2,2048,1408]{2,1,0:T(8,128)(2,1)} %all-gather.14.cloned.1.call-done) | copy-start | bytes 34603012
  424.9 26.7 %slice-start = ((s8[11534336]{0:T(1024)(128)(4,1)}), s8[3145728]{0:T(1024)(128)(4,1)S(1)}, s32[]{:S(2)}) async-start(s8[11534336]{0:T(1024)(128)(4,1)} %bitcast.200), calls=%async_computation.24 | async-start | bytes 6291456
  425.0 26.7 %slice-start.1 = ((s8[11534336]{0:T(1024)(128)(4,1)}), s8[4194304]{0:T(1024)(128)(4,1)S(1)}, s32[]{:S(2)}) async-start(s8[11534336]{0:T(1024)(128)(4,1)} %bitcast.200), calls=%async_computation.25 | async-start | bytes 8388608
  441.9 9.8 %slice-start.2 = ((s8[11534336]{0:T(1024)(128)(4,1)}), s8[4194304]{0:T(1024)(128)(4,1)S(1)}, s32[]{:S(2)}) async-start(s8[11534336]{0:T(1024)(128)(4,1)} %bitcast.200), calls=%async_computation.26 | async-start | bytes 8388608
  461.8 262.7 %reduce-scatter.29.cloned.1.call-start = ((), (), s32[]{:S(2)}) async-start(), calls=%async_computation.22 | async-start | bytes 6488064 | tf_op jit(solution)/shard_map/reduce_scatter | solution.py:236
  472.4 254.6 %reduce-scatter.25.cloned.1.call-start = ((), (), s32[]{:S(2)}) async-start(), calls=%async_computation.20 | async-start | bytes 6488064 | tf_op jit(solution)/shard_map/reduce_scatter | solution.py:230
  484.0 243.0 %reduce-scatter.27.cloned.1.call-start = ((), (), s32[]{:S(2)}) async-start(), calls=%async_computation.21 | async-start | bytes 6488064 | tf_op jit(solution)/shard_map/reduce_scatter | solution.py:233
  512.8 8.2 copy-start.13
  512.8 8.2 copy-start.54
  515.8 13.8 %copy-start.44 = (f32[256]{0:T(256)}, f32[256]{0:T(256)S(1)}, u32[]{:S(2)}) copy-start(f32[256]{0:T(256)S(1)} %broadcast_multiply_fusion.2) | copy-start | bytes 3076
  515.8 13.7 %copy-start.46 = (f32[256]{0:T(256)}, f32[256]{0:T(256)S(1)}, u32[]{:S(2)}) copy-start(f32[256]{0:T(256)S(1)} %broadcast_multiply_fusion.3) | copy-start | bytes 3076
  519.5 24.9 %collective-permute-start.6 = (bf16[256,2048]{1,0:T(8,128)(2,1)}, bf16[256,2048]{1,0:T(8,128)(2,1)S(1)}, u32[]{:S(2)}, u32[]{:S(2)}) collective-permute-start(bf16[256,2048]{1,0:T(8,128)(2,1)} %fusion.107), channel_id=1, source_target_pairs={{0,3},{1,0},{2,1},{3,2},{4,7},{5,4},{6,5},{7,6},{8,11},{9,8},{10,9... | collective-permute-start | bytes 3145736 | tf_op jit(solution)/shard_map/ppermute | solution.py:17
  529.6 213.2 %reduce-scatter.31.cloned.1.call-start = ((), (), s32[]{:S(2)}) async-start(), calls=%async_computation.23 | async-start | bytes 147456
  547.2 46.7 %collective-permute-start.7 = (bf16[512,2048]{1,0:T(8,128)(2,1)}, bf16[512,2048]{1,0:T(8,128)(2,1)}, u32[]{:S(2)}, u32[]{:S(2)}) collective-permute-start(bf16[512,2048]{1,0:T(8,128)(2,1)} %pad_maximum_fusion.3), channel_id=1, source_target_pairs={{0,2},{1,3},{2,0},{3,1},{4,6},{5,7},{6,4},{7,5},{8,10},{9,11},{10,... | collective-permute-start | bytes 6291464 | tf_op jit(solution)/shard_map/ppermute | solution.py:17
  548.7 58.0 %copy-start.50 = (bf16[512,2048]{1,0:T(8,128)(2,1)S(1)}, bf16[512,2048]{1,0:T(8,128)(2,1)}, u32[]{:S(2)}) copy-start(bf16[512,2048]{1,0:T(8,128)(2,1)} %all-gather.12.cloned.1.call-done) | copy-start | bytes 6291460
  613.9 4.1 copy-start.25
  627.8 4.0 copy-start.20
  627.8 4.0 copy-start.23
  635.3 4.1 copy-start.25
  649.1 3.9 copy-start.20
  656.5 5.0 copy-start.18
  659.8 4.2 copy-start.30
  659.8 4.2 copy-start.32
  682.8 97.1 %reduce-scatter.23.cloned.1.call-start = ((), (), s32[]{:S(2)}) async-start(), calls=%async_computation.19 | async-start | bytes 2359296 | tf_op jit(solution)/shard_map/reduce_scatter | solution.py:316
  689.1 144.8 %reduce-scatter.19.cloned.1.call-start = ((), (), s32[]{:S(2)}) async-start(), calls=%async_computation.17 | async-start | bytes 5242880 | tf_op jit(solution)/shard_map/reduce_scatter | solution.py:103
  700.3 189.4 %reduce-scatter.15.cloned.1.call-start = ((), (), s32[]{:S(2)}) async-start(), calls=%async_computation.15 | async-start | bytes 5242880 | tf_op jit(solution)/shard_map/reduce_scatter | solution.py:103
  711.4 250.2 %reduce-scatter.21.cloned.1.call-start = ((), (), s32[]{:S(2)}) async-start(), calls=%async_computation.18 | async-start | bytes 7077888 | tf_op jit(solution)/shard_map/reduce_scatter | solution.py:310
  724.5 110.8 %copy-start.1 = (bf16[256,2048]{1,0:T(8,128)(2,1)S(1)}, bf16[256,2048]{1,0:T(8,128)(2,1)}, u32[]{:S(2)}) copy-start(bf16[256,2048]{1,0:T(8,128)(2,1)} %param.17) | copy-start | bytes 3145732
  724.5 110.8 %copy-start.34 = (f32[8,1,256]{2,1,0:T(1,128)S(1)}, f32[8,1,256]{2,1,0:T(1,128)}, u32[]{:S(2)}) copy-start(f32[8,1,256]{2,1,0:T(1,128)} %copy-done.33) | copy-start | bytes 24580
  724.5 110.8 %copy-start.38 = (f32[256]{0:T(256)S(1)}, f32[256]{0:T(256)}, u32[]{:S(2)}) copy-start(f32[256]{0:T(256)} %copy-done.37) | copy-start | bytes 3076
  724.5 110.8 %copy-start.43 = (f32[256]{0:T(256)S(1)}, f32[256]{0:T(256)}, u32[]{:S(2)}) copy-start(f32[256]{0:T(256)} %copy-done.42) | copy-start | bytes 3076
  727.0 110.6 %copy-start.41 = (bf16[2048]{0:T(1024)(128)(2,1)S(1)}, bf16[2048]{0:T(1024)(128)(2,1)}, u32[]{:S(2)}) copy-start(bf16[2048]{0:T(1024)(128)(2,1)} %get-tuple-element.258) | copy-start | bytes 12292
  727.0 162.7 %copy-start.7 = (bf16[256,2048]{1,0:T(8,128)(2,1)S(1)}, bf16[256,2048]{1,0:T(8,128)(2,1)}, u32[]{:S(2)}) copy-start(bf16[256,2048]{1,0:T(8,128)(2,1)} %reduce-scatter.13.cloned.1.call-done) | copy-start | bytes 3145732
  727.0 162.7 %copy-start.28 = (f32[8,1,256]{2,1,0:T(1,128)S(1)}, f32[8,1,256]{2,1,0:T(1,128)}, u32[]{:S(2)}) copy-start(f32[8,1,256]{2,1,0:T(1,128)} %copy-done.27) | copy-start | bytes 24580
  727.0 162.7 %copy-start.36 = (f32[256]{0:T(256)S(1)}, f32[256]{0:T(256)}, u32[]{:S(2)}) copy-start(f32[256]{0:T(256)} %copy-done.35) | copy-start | bytes 3076
  727.0 162.7 %copy-start.40 = (f32[256]{0:T(256)S(1)}, f32[256]{0:T(256)}, u32[]{:S(2)}) copy-start(f32[256]{0:T(256)} %copy-done.39) | copy-start | bytes 3076
  727.0 162.7 %copy-start.45 = (f32[256]{0:T(256)S(1)}, f32[256]{0:T(256)}, u32[]{:S(2)}) copy-start(f32[256]{0:T(256)} %copy-done.44) | copy-start | bytes 3076
  727.0 162.7 %copy-start.47 = (f32[256]{0:T(256)S(1)}, f32[256]{0:T(256)}, u32[]{:S(2)}) copy-start(f32[256]{0:T(256)} %copy-done.46) | copy-start | bytes 3076
  (31 other events, 66.9 us)
Sparse Core Ops, SparseCore 0:
  9.6 67.4 all-gather.9
  78.7 29.2 all-gather.11
  184.4 70.3 reduce-scatter.12
  256.3 108.0 all-gather.13
  365.8 59.0 all-gather.15
  461.9 50.7 reduce-scatter.16
  515.1 64.7 reduce-scatter.28
  582.2 63.2 reduce-scatter.24
  647.8 63.2 reduce-scatter.26
  713.7 29.0 reduce-scatter.30
  745.7 34.1 reduce-scatter.22
  782.7 51.1 reduce-scatter.18
  836.9 52.7 reduce-scatter.14
  891.8 69.7 reduce-scatter.20
